TPU v7x, 32 devices: a whole 2x2x4 slice. The times are simulated.
32 devices in a mesh: sec: 2 (over core), req: 4 (over z), head: 4 (over y, x).
Axes of the slice: x: 2, y: 2, z: 4, core: 2. Of those that a mesh axis runs over, the one named last changes fastest.
Arguments:
- queries: bfloat16 [32, 32, 4096], P(('sec', 'req'), None, 'head'), as said below
- tree_keys: bfloat16 [32, 32, 512], P(('sec', 'req'), None, 'head'), may hold values from -4 to 4
- tree_values: bfloat16 [32, 32, 512], P(('sec', 'req'), None, 'head'), may hold values from -4 to 4
- cache_keys: bfloat16 [32, 4, 4096, 128], P(('sec', 'req'), 'head'), as said below
- cache_values: bfloat16 [32, 4, 4096, 128], P(('sec', 'req'), 'head'), may hold values from -4 to 4
- cache_lengths: int32 [32], P(('sec', 'req')), may hold values from 1024 to 4096
- tree_parents: int32 [32, 32], P(('sec', 'req')), may hold values from 0 to 30, as said below
- out_weight: bfloat16 [4096, 2048], P('head'), may hold values from -0.09375 to 0.09375
- hidden: bfloat16 [1024, 2048], P(('sec', 'req', 'head')), may hold values from -0.1796875 to 0.1796875
- norm_gain: float32 [2048], replicated, may hold values from 0.1 to 1.9
- expert_ids: int32 [1024, 8], P(('sec', 'req', 'head')), may hold values from 0 to 31, all different within a row; in each aligned block of 32 rows (0 to 31, 32 to 63, ...) at most 16 rows name the same one
- route_weights: float32 [1024, 8], P(('sec', 'req', 'head')), may hold values from 0.05 to 0.25
- expert_gate_up: bfloat16 [32, 2048, 1536], P(('sec', 'req', 'head')), may hold values from -0.125 to 0.125
- expert_down: bfloat16 [32, 768, 2048], P(('sec', 'req', 'head')), may hold values from -0.21875 to 0.21875
Outputs:
- layer_out: bfloat16 [1024, 2048], P(('sec', 'req', 'head'))
Inputs may be any that keep to these rules, and one draw needn't show every extreme that they name: `queries`: values lie within -4.5 to 4.5. `cache_keys`: values lie within -4.5 to 4.5. tree_parents[r, i] < i for i >= 1, and tree_parents[r, 0] = 0. `expert_ids`: each row names 8 different experts. Among the 32 rows of one device (aligned blocks of rows), no expert is named more than 16 times, a bound that some block reaches.
All inputs are finite; a program needn't handle non-finite values.
Results may differ from a plain program's by a relative error of at most 0.02.
Values may be sent and summed in bfloat16 or wider, within the bound.
A program may use at most 128 MiB of HBM per device.

v0:
```python
import functools
import math

import jax
import jax.numpy as jnp
from jax import lax
from jax.experimental import pallas as pl
from jax.experimental.pallas import tpu as pltpu
from jax.sharding import PartitionSpec as P

F32 = jnp.float32
BF16 = jnp.bfloat16
NEG = -1e30
CHUNKS = (2048, 512)
LANES = 128


def dot_nt(a, b):
    return lax.dot_general(a, b, (((1,), (1,)), ((), ())), preferred_element_type=F32)


def dot_nn(a, b):
    return jnp.dot(a, b, preferred_element_type=F32)


def attend_kernel(
    len_ref, q_ref, tk_ref, tv_ref, par_ref, ck_ref, cv_ref, wo_hbm, out_ref,
    attended, m_ref, l_ref, acc_ref, wo_ref, wo_sem,
):
    r = pl.program_id(0)
    last = pl.num_programs(0) - 1
    weights = pltpu.make_async_copy(wo_hbm, wo_ref, wo_sem)

    @pl.when(r == 0)
    def _():
        weights.start()

    tree, width = q_ref.shape[1:]
    hd = ck_ref.shape[3]
    cache = ck_ref.shape[2]
    groups = width // hd
    scale = hd ** (-0.5) * math.log2(math.e)
    q = q_ref[0]
    rows = jnp.concatenate([q[:, g * hd : (g + 1) * hd] for g in range(groups)], axis=0)

    down = lax.broadcasted_iota(jnp.int32, (tree, tree), 0)
    across = lax.broadcasted_iota(jnp.int32, (tree, tree), 1)
    eye = (down == across).astype(F32)
    linked_t = (jnp.broadcast_to(par_ref[0], (tree, tree)) == down).astype(F32)
    closure = jnp.minimum(dot_nt(eye.astype(BF16), linked_t.astype(BF16)) + eye, 1.0)
    for _ in range(max(1, (tree - 1).bit_length())):
        half = closure.astype(BF16)
        closure = jnp.minimum(dot_nn(half, half), 1.0)
    admitted = jnp.concatenate([closure] * groups, axis=0)

    scores = jnp.where(admitted > 0.5, dot_nt(rows, tk_ref[0]) * scale, NEG)
    highest = jnp.max(scores, -1, keepdims=True)
    probs = jnp.exp2(scores - highest)
    m_ref[...] = jnp.broadcast_to(highest, m_ref.shape)
    l_ref[...] = jnp.broadcast_to(jnp.sum(probs, -1, keepdims=True), l_ref.shape)
    acc_ref[...] = dot_nn(probs.astype(BF16), tv_ref[0])

    length = len_ref[r]

    def step(start, chunk, masked):
        start = pl.multiple_of(start, chunk)
        s = dot_nt(rows, ck_ref[0, 0, pl.ds(start, chunk), :]) * scale
        if masked:
            place = lax.broadcasted_iota(jnp.int32, s.shape, 1)
            s = jnp.where(place < length - start, s, NEG)
        before = m_ref[:, :1]
        now = jnp.maximum(before, jnp.max(s, -1, keepdims=True))
        p = jnp.exp2(s - now)
        fade = jnp.exp2(before - now)
        l_ref[...] = l_ref[...] * fade + jnp.sum(p, -1, keepdims=True)
        acc_ref[...] = acc_ref[...] * fade + dot_nn(
            p.astype(BF16), cv_ref[0, 0, pl.ds(start, chunk), :]
        )
        m_ref[...] = jnp.broadcast_to(now, m_ref.shape)

    done = 0
    for chunk in CHUNKS:
        assert cache % chunk == 0
        upto = length // chunk

        @pl.loop(done // chunk, upto)
        def _(i, chunk=chunk):
            step(i * chunk, chunk, False)

        done = upto * chunk

    @pl.when(done < length)
    def _():
        step(done, CHUNKS[-1], True)

    o = (acc_ref[...] / l_ref[:, :1]).astype(BF16)
    for g in range(groups):
        attended[r, :, g * hd : (g + 1) * hd] = o[g * tree : (g + 1) * tree]

    @pl.when(r == last)
    def _():
        weights.wait()
        a = attended[...].reshape(-1, width)
        out_ref[...] = dot_nn(a, wo_ref[...]).astype(BF16)


def attend(queries, tree_keys, tree_values, cache_keys, cache_values, lengths, parents, out_weight):
    req, tree, width = queries.shape
    cache, hd = cache_keys.shape[2:]
    assert cache_keys.shape[1] == 1
    model = out_weight.shape[1]
    rows = tree * (width // hd)
    grid_spec = pltpu.PrefetchScalarGridSpec(
        num_scalar_prefetch=1,
        grid=(req,),
        in_specs=[
            pl.BlockSpec((1, tree, width), lambda r, n: (r, 0, 0)),
            pl.BlockSpec((1, tree, hd), lambda r, n: (r, 0, 0)),
            pl.BlockSpec((1, tree, hd), lambda r, n: (r, 0, 0)),
            pl.BlockSpec((1, 1, tree), lambda r, n: (r, 0, 0)),
            pl.BlockSpec((1, 1, cache, hd), lambda r, n: (r, 0, 0, 0)),
            pl.BlockSpec((1, 1, cache, hd), lambda r, n: (r, 0, 0, 0)),
            pl.BlockSpec(memory_space=pl.ANY),
        ],
        out_specs=pl.BlockSpec((req * tree, model), lambda r, n: (0, 0)),
        scratch_shapes=[
            pltpu.VMEM((req, tree, width), BF16),
            pltpu.VMEM((rows, LANES), F32),
            pltpu.VMEM((rows, LANES), F32),
            pltpu.VMEM((rows, hd), F32),
            pltpu.VMEM(out_weight.shape, BF16),
            pltpu.SemaphoreType.DMA,
        ],
    )
    return pl.pallas_call(
        attend_kernel,
        grid_spec=grid_spec,
        out_shape=jax.ShapeDtypeStruct((req * tree, model), BF16),
        compiler_params=pltpu.CompilerParams(
            dimension_semantics=("arbitrary",), vmem_limit_bytes=67043328
        ),
    )(lengths, queries, tree_keys, tree_values, parents.reshape(req, 1, tree), cache_keys,
      cache_values, out_weight)


def copy_count(z_n, y_n, x_n):
    gather = 2 * (z_n - 1) + z_n * (x_n * y_n - 1) * 2 + 2 * z_n
    back = 2 * z_n + 2 * z_n * (y_n - 1 + x_n - 1) + 2 * (z_n - 1)
    return (y_n * x_n - 1) + gather + back


def expert_kernel(
    dims, part_ref, hid_ref, gain_ref, ids_ref, rw_ref, gu_hbm, dn_hbm, out_ref,
    head_in, bank, sums, pair_in, first_in, second_in, z_in, resid_ref, gu, dn,
    send, recv, load_sem,
):
    z_n, y_n, x_n = dims
    h_n = y_n * x_n
    s = lax.axis_index("sec")
    z = lax.axis_index("req")
    h = lax.axis_index("head")
    y = h // x_n
    x = h % x_n
    tok, model = hid_ref.shape
    half = model // 2
    mine = (s * z_n + z) * h_n + h

    def to_head(k):
        return {"head": lax.rem(h + k, h_n)}

    def to_z(k):
        return {"req": lax.rem(z + k, z_n)}

    def to_yx(dy, dx):
        return {"head": lax.rem(y + dy, y_n) * x_n + lax.rem(x + dx, x_n)}

    partner = {"sec": 1 - s}
    barrier = pltpu.get_barrier_semaphore()
    peers = [to_head(k) for k in range(1, h_n)] + [to_z(k) for k in range(1, z_n)] + [partner]
    for peer in peers:
        pl.semaphore_signal(
            barrier, inc=1, device_id=peer, device_id_type=pl.DeviceIdType.MESH
        )
    load_gu = pltpu.make_async_copy(gu_hbm.at[0], gu, load_sem.at[0])
    load_dn = pltpu.make_async_copy(dn_hbm.at[0], dn, load_sem.at[1])
    load_gu.start()
    load_dn.start()
    pl.semaphore_wait(barrier, len(peers))

    made = []

    def push(src, dst, peer):
        k = len(made)
        c = pltpu.make_async_remote_copy(
            src_ref=src, dst_ref=dst, send_sem=send.at[k], recv_sem=recv.at[k],
            device_id=peer, device_id_type=pl.DeviceIdType.MESH,
        )
        made.append(c)
        c.start()
        return c

    arrivals = []
    for k in range(1, h_n):
        row = pl.multiple_of(lax.rem(h + k, h_n) * tok, tok)
        arrivals.append(push(part_ref.at[pl.ds(row, tok), :], head_in.at[k - 1], to_head(k)))
    lanes = bank.shape[-1] - half
    labels = lax.broadcasted_iota(jnp.int32, (lanes, tok), 0)
    dense = jnp.zeros((lanes, tok), F32)
    for k in range(ids_ref.shape[0]):
        dense = dense + jnp.where(ids_ref[k : k + 1, :] == labels, rw_ref[k : k + 1, :], 0.0)
    high = dense.astype(BF16)
    low = (dense - high.astype(F32)).astype(BF16)
    eye = (
        lax.broadcasted_iota(jnp.int32, (tok, tok), 0)
        == lax.broadcasted_iota(jnp.int32, (tok, tok), 1)
    ).astype(F32).astype(BF16)
    high = dot_nt(eye, high).astype(BF16)
    low = dot_nt(eye, low).astype(BF16)
    own_row = pl.multiple_of(h * tok, tok)
    resid = hid_ref[...].astype(F32) + part_ref[pl.ds(own_row, tok), :].astype(F32)
    for k in range(1, h_n):
        arrivals[k - 1].wait_recv()
        resid = resid + head_in[k - 1].astype(F32)
    resid_ref[...] = resid
    normed = (
        resid * lax.rsqrt(jnp.mean(resid * resid, -1, keepdims=True) + 1e-06) * gain_ref[...]
    ).astype(BF16)
    for f, extra in ((0, high), (1, low)):
        bank[0, f, 0, 0, 0, :, :half] = normed[:, f * half : (f + 1) * half]
        bank[0, f, 0, 0, 0, :, half:] = extra

    got = {}

    def gather(f, dz, dy, dx, src, peer):
        got[f, dz, dy, dx] = push(
            bank.at[(0, f, dz) + src], bank.at[0, f, dz, dy, dx], peer
        )

    for dz in range(1, z_n):
        for f in range(2):
            got[f, dz, 0, 0] = push(bank.at[0, f, 0, 0, 0], bank.at[0, f, dz, 0, 0], to_z(dz))

    def stage_a(dz):
        for f in range(2):
            if dz:
                got[f, dz, 0, 0].wait_recv()
            for dx in range(1, x_n):
                gather(f, dz, 0, dx, (0, 0), to_yx(0, dx)) if f == 0 else None
            for dy in range(1, y_n):
                gather(f, dz, dy, 0, (0, 0), to_yx(dy, 0)) if f == 1 else None
        for dy in range(1, y_n):
            gather(0, dz, dy, 0, (0, 0), to_yx(dy, 0))
        for dx in range(1, x_n):
            gather(1, dz, 0, dx, (0, 0), to_yx(0, dx))

    def stage_b(dz):
        for dx in range(1, x_n):
            got[0, dz, 0, dx].wait_recv()
            for dy in range(1, y_n):
                gather(0, dz, dy, dx, (0, dx), to_yx(dy, 0))
        for dy in range(1, y_n):
            got[1, dz, dy, 0].wait_recv()
            for dx in range(1, x_n):
                gather(1, dz, dy, dx, (dy, 0), to_yx(0, dx))

    crossed = {}

    def stage_c(dz):
        for f in range(2):
            for dy in range(y_n):
                for dx in range(x_n):
                    seen = (dy == 0 and dx == 0) or (f == 0 and dy == 0) or (f == 1 and dx == 0)
                    if not seen:
                        got[f, dz, dy, dx].wait_recv()
            crossed[f, dz] = push(bank.at[0, f, dz], bank.at[1, f, dz], partner)

    count = 2 * h_n * tok
    apart = 1 if h_n * tok <= 128 else y_n

    def experts(dz):
        for f in range(2):
            crossed[f, dz].wait_recv()
        pick = lax.broadcasted_iota(jnp.int32, (1, lanes), 1) == mine
        for part in range(apart):
            ys = slice(part * (y_n // apart), (part + 1) * (y_n // apart))
            left = bank[:, 0, dz, ys].reshape(count // apart, half + lanes)
            right = bank[:, 1, dz, ys].reshape(count // apart, half + lanes)
            named = left[:, half:].astype(F32) + right[:, half:].astype(F32)
            weight = jnp.sum(jnp.where(pick, named, 0.0), -1, keepdims=True)
            mixed = dot_nn(left[:, :half], gu[:half]) + dot_nn(right[:, :half], gu[half:])
            hidden = mixed.shape[1] // 2
            gate = mixed[:, :hidden]
            active = (gate / (1.0 + jnp.exp(-gate)) * mixed[:, hidden:]).astype(BF16)
            result = jnp.where(weight > 0.0, dot_nn(active, dn[...]) * weight, 0.0).astype(BF16)
            shaped = result.reshape(2, y_n // apart, x_n, tok, model)
            for f in range(2):
                sums[f, dz, ys] = shaped[0, ..., f * half : (f + 1) * half]
                bank[1, f, dz, ys, :, :, :half] = shaped[1, ..., f * half : (f + 1) * half]

    paired, firsts, seconds, ends = {}, {}, {}, {}

    def back_pair(dz):
        for f in range(2):
            paired[f, dz] = push(
                bank.at[1, f, dz, :, :, :, pl.ds(0, half)], pair_in.at[f, dz], partner
            )

    def back_first(dz):
        for f in range(2):
            paired[f, dz].wait_recv()
            sums[f, dz] = (sums[f, dz].astype(F32) + pair_in[f, dz].astype(F32)).astype(BF16)
            if f == 0:
                for dy in range(1, y_n):
                    firsts[f, dz, dy] = push(
                        sums.at[f, dz, dy], first_in.at[f, dz, dy - 1], to_yx(y_n - dy, 0)
                    )
            else:
                for dx in range(1, x_n):
                    firsts[f, dz, dx] = push(
                        sums.at[f, dz, :, dx], first_in.at[f, dz, dx - 1], to_yx(0, x_n - dx)
                    )

    def back_second(dz):
        for f in range(2):
            total = sums[f, dz, 0] if f == 0 else sums[f, dz, :, 0]
            total = total.astype(F32)
            for d in range(1, y_n if f == 0 else x_n):
                firsts[f, dz, d].wait_recv()
                total = total + first_in[f, dz, d - 1].astype(F32)
            if f == 0:
                sums[f, dz, 0] = total.astype(BF16)
                for dx in range(1, x_n):
                    seconds[f, dz, dx] = push(
                        sums.at[f, dz, 0, dx], second_in.at[f, dz, dx - 1], to_yx(0, x_n - dx)
                    )
            else:
                sums[f, dz, :, 0] = total.astype(BF16)
                for dy in range(1, y_n):
                    seconds[f, dz, dy] = push(
                        sums.at[f, dz, dy, 0], second_in.at[f, dz, dy - 1], to_yx(y_n - dy, 0)
                    )

    def back_end(dz):
        for f in range(2):
            total = sums[f, dz, 0, 0].astype(F32)
            for d in range(1, x_n if f == 0 else y_n):
                seconds[f, dz, d].wait_recv()
                total = total + second_in[f, dz, d - 1].astype(F32)
            if dz:
                sums[f, dz, 0, 0] = total.astype(BF16)
                ends[f, dz] = push(sums.at[f, dz, 0, 0], z_in.at[f, dz - 1], to_z(z_n - dz))
            else:
                cols = slice(f * half, (f + 1) * half)
                resid_ref[:, cols] = resid_ref[:, cols] + total

    order = list(range(1, z_n)) + [0]

    def back(j):
        for stage, lag in ((back_end, 3), (back_second, 2), (back_first, 1)):
            if 0 <= j - lag < z_n:
                stage(order[j - lag])

    ran = 0
    for i in range(z_n + 2):
        for stage, lag in ((stage_a, 0), (stage_b, 1), (stage_c, 2)):
            if 0 <= i - lag < z_n:
                stage(i - lag)
        if i == 2:
            load_gu.wait()
            load_dn.wait()
        while ran < z_n and (i == z_n + 1 or order[ran] <= i - 2 and order[ran] > 0):
            experts(order[ran])
            back_pair(order[ran])
            back(ran)
            ran += 1
    for j in range(z_n, z_n + 3):
        back(j)
    for f in range(2):
        cols = slice(f * half, (f + 1) * half)
        total = resid_ref[:, cols]
        for dz in range(1, z_n):
            ends[f, dz].wait_recv()
            total = total + z_in[f, dz - 1].astype(F32)
        out_ref[:, cols] = total.astype(BF16)
    for c in made:
        c.wait_send()
    assert len(made) == copy_count(*dims)


def expert_layer(dims, partial, hidden, gain, ids, route, gate_up, down):
    z_n, y_n, x_n = dims
    tok, model = hidden.shape
    half = model // 2
    experts = gate_up.shape[0] * 2 * z_n * y_n * x_n
    assert gate_up.shape[0] == 1 and partial.shape[0] == y_n * x_n * tok
    lanes = -(-experts // LANES) * LANES
    most = max(y_n, x_n)
    copies = copy_count(*dims)
    vmem = pl.BlockSpec(memory_space=pltpu.VMEM)
    return pl.pallas_call(
        functools.partial(expert_kernel, dims),
        out_shape=jax.ShapeDtypeStruct((tok, model), BF16),
        in_specs=[vmem] * 5 + [pl.BlockSpec(memory_space=pl.ANY)] * 2,
        out_specs=vmem,
        scratch_shapes=[
            pltpu.VMEM((y_n * x_n - 1, tok, model), BF16),
            pltpu.VMEM((2, 2, z_n, y_n, x_n, tok, half + lanes), BF16),
            pltpu.VMEM((2, z_n, y_n, x_n, tok, half), BF16),
            pltpu.VMEM((2, z_n, y_n, x_n, tok, half), BF16),
            pltpu.VMEM((2, z_n, most - 1, most, tok, half), BF16),
            pltpu.VMEM((2, z_n, most - 1, tok, half), BF16),
            pltpu.VMEM((2, z_n - 1, tok, half), BF16),
            pltpu.VMEM((tok, model), F32),
            pltpu.VMEM(gate_up.shape[1:], BF16),
            pltpu.VMEM(down.shape[1:], BF16),
            pltpu.SemaphoreType.DMA((copies,)),
            pltpu.SemaphoreType.DMA((copies,)),
            pltpu.SemaphoreType.DMA((2,)),
        ],
        compiler_params=pltpu.CompilerParams(
            collective_id=0, has_side_effects=True, vmem_limit_bytes=67043328
        ),
    )(partial, hidden, gain.reshape(1, -1), ids.T, route.T, gate_up, down)


def per_device(
    dims, queries, tree_keys, tree_values, cache_keys, cache_values, cache_lengths, tree_parents,
    out_weight, hidden, norm_gain, expert_ids, route_weights, expert_gate_up, expert_down,
):
    partial = attend(
        queries, tree_keys, tree_values, cache_keys, cache_values, cache_lengths, tree_parents,
        out_weight,
    )
    return expert_layer(
        dims, partial, hidden, norm_gain, expert_ids, route_weights, expert_gate_up, expert_down
    )


def solution(mesh):
    heads = mesh.shape["head"]
    x_n = math.isqrt(heads)
    while heads % x_n:
        x_n -= 1
    assert mesh.shape["sec"] == 2
    dims = (mesh.shape["req"], heads // x_n, x_n)
    tokens = ("sec", "req", "head")
    in_specs = (
        P(("sec", "req"), None, "head"),
        P(("sec", "req"), None, "head"),
        P(("sec", "req"), None, "head"),
        P(("sec", "req"), "head", None, None),
        P(("sec", "req"), "head", None, None),
        P(("sec", "req")),
        P(("sec", "req"), None),
        P("head", None),
        P(tokens, None),
        P(),
        P(tokens, None),
        P(tokens, None),
        P(tokens, None, None),
        P(tokens, None, None),
    )
    return jax.shard_map(
        functools.partial(per_device, dims), mesh=mesh, in_specs=in_specs,
        out_specs=P(tokens, None), check_vma=False,
    )
```

profile of v0, /device:TPU:0, one launch (start us, length us, event | category | flops | bytes accessed | tf_op | source)
XLA Modules:
  0.0 94.2 jit_solution(2834547460365289319)
XLA Ops:
  0.0 19.3 %shard_map.136.part_ref = bf16[128,2048]{1,0:T(8,128)(2,1)} custom-call(s32[4]{0:T(128)} %len_ref.1, bf16[4,32,1024]{2,1,0:T(8,128)(2,1)} %q_ref.1, bf16[4,32,128]{2,1,0:T(8,128)(2,1)} %tk_ref.1, bf16[4,32,128]{2,1,0:T(8,128)(2,1)} %tv_ref.1, s32[4,1,32]{2,1,0:T(1,128)} %bitcast.9, bf16[4,1,4096,128]{3,2,1,0:T(8,128)(2,1)} %ck_ref.1, ...), custom_call_target="tpu_custom_call" | custom-call | tf_op jit(solution)/shard_map/pallas_call | solution.py:135
  19.3 73.3 %shard_map.137 = bf16[32,2048]{1,0:T(8,128)(2,1)} custom-call(bf16[128,2048]{1,0:T(8,128)(2,1)} %shard_map.136.part_ref, bf16[32,2048]{1,0:T(8,128)(2,1)} %hid_ref.1, f32[1,2048]{1,0:T(1,128)} %bitcast.6, s32[8,32]{1,0:T(8,128)} %bitcast.7, f32[8,32]{1,0:T(8,128)} %bitcast.8, bf16[1,2048,1536]{2,1,0:T(8,128)(2,1)} %gu_hbm.1, bf16[1,768,2048]{2,1,0:T(8,128)(2,1)} %dn_hbm.1), custom_call_target="tpu_custom_call" | custom-call | tf_op jit(solution)/shard_map/pallas_call | solution.py:400
  92.6 1.6 %copy.17 = bf16[32,2048]{1,0:T(8,128)(2,1)} copy(bf16[32,2048]{1,0:T(8,128)(2,1)} %shard_map.137) | data formatting | bytes 262144
where the time goes:
time: 93.9 us; the launch traced here: 94.2 us
  Pallas kernels  92.6 us (99%)
  local copies, waits for them, and re-layouts  1.57 us (2%)
    pallas_call x1, Pallas kernels, expert_layer(): pl.pallas_call(functools.partial(expert_kernel, dims), out_shape=jax.Shap...  73.3 us
    pallas_call x1, Pallas kernels, attend(): pl.pallas_call(attend_kernel, grid_spec=grid_spec, out_shape=jax.ShapeDty...  19.3 us

commit v1 on v0

--- a/solution.py
+++ b/solution.py
@@ -144,7 +144,7 @@
 
 
 def copy_count(z_n, y_n, x_n):
-    gather = 2 * (z_n - 1) + z_n * (x_n * y_n - 1) * 2 + 2 * z_n
+    gather = 2 * (z_n - 1) + z_n * (x_n * y_n - 1) * 2 + 2 * z_n * y_n * x_n
     back = 2 * z_n + 2 * z_n * (y_n - 1 + x_n - 1) + 2 * (z_n - 1)
     return (y_n * x_n - 1) + gather + back
 
@@ -240,10 +240,18 @@
         for f in range(2):
             got[f, dz, 0, 0] = push(bank.at[0, f, 0, 0, 0], bank.at[0, f, dz, 0, 0], to_z(dz))
 
+    crossed = {}
+
+    def cross(f, dz, dy, dx):
+        crossed[f, dz, dy, dx] = push(
+            bank.at[0, f, dz, dy, dx], bank.at[1, f, dz, dy, dx], partner
+        )
+
     def stage_a(dz):
         for f in range(2):
             if dz:
                 got[f, dz, 0, 0].wait_recv()
+            cross(f, dz, 0, 0)
             for dx in range(1, x_n):
                 gather(f, dz, 0, dx, (0, 0), to_yx(0, dx)) if f == 0 else None
             for dy in range(1, y_n):
@@ -258,12 +266,12 @@
             got[0, dz, 0, dx].wait_recv()
             for dy in range(1, y_n):
                 gather(0, dz, dy, dx, (0, dx), to_yx(dy, 0))
+            cross(0, dz, 0, dx)
         for dy in range(1, y_n):
             got[1, dz, dy, 0].wait_recv()
             for dx in range(1, x_n):
                 gather(1, dz, dy, dx, (dy, 0), to_yx(0, dx))
-
-    crossed = {}
+            cross(1, dz, dy, 0)
 
     def stage_c(dz):
         for f in range(2):
@@ -272,14 +280,16 @@
                     seen = (dy == 0 and dx == 0) or (f == 0 and dy == 0) or (f == 1 and dx == 0)
                     if not seen:
                         got[f, dz, dy, dx].wait_recv()
-            crossed[f, dz] = push(bank.at[0, f, dz], bank.at[1, f, dz], partner)
+                        cross(f, dz, dy, dx)
 
     count = 2 * h_n * tok
     apart = 1 if h_n * tok <= 128 else y_n
 
     def experts(dz):
         for f in range(2):
-            crossed[f, dz].wait_recv()
+            for dy in range(y_n):
+                for dx in range(x_n):
+                    crossed[f, dz, dy, dx].wait_recv()
         pick = lax.broadcasted_iota(jnp.int32, (1, lanes), 1) == mine
         for part in range(apart):
             ys = slice(part * (y_n // apart), (part + 1) * (y_n // apart))

time: 93.9 us -> 92.6 us (0.986)
  Pallas kernels: 92.6 us -> 90.5 us
    pallas_call x1, Pallas kernels: 19.3 us -> 16.3 us  [attend(): pl.pallas_call(attend_kernel, grid_spec=grid_spec, out_shape=jax.ShapeDty...]
    pallas_call x1, Pallas kernels: 73.3 us -> 74.3 us  [expert_layer(): pl.pallas_call(functools.partial(expert_kernel, dims), out_shape=jax.Shap...]
where the time goes in v1:
time: 92.6 us; the launch traced here: 92.1 us
  Pallas kernels  90.5 us (98%)
  local copies, waits for them, and re-layouts  1.57 us (2%)
    pallas_call x1, Pallas kernels, expert_layer(): pl.pallas_call(functools.partial(expert_kernel, dims), out_shape=jax.Shap...  74.3 us
    pallas_call x1, Pallas kernels, attend(): pl.pallas_call(attend_kernel, grid_spec=grid_spec, out_shape=jax.ShapeDty...  16.3 us

profile of v1, /device:TPU:0, one launch (start us, length us, event | category | flops | bytes accessed | tf_op | source)
XLA Modules:
  0.0 92.1 jit_solution(3254530599383489505)
XLA Ops:
  0.0 16.3 %shard_map.136.part_ref = bf16[128,2048]{1,0:T(8,128)(2,1)} custom-call(s32[4]{0:T(128)} %len_ref.1, bf16[4,32,1024]{2,1,0:T(8,128)(2,1)} %q_ref.1, bf16[4,32,128]{2,1,0:T(8,128)(2,1)} %tk_ref.1, bf16[4,32,128]{2,1,0:T(8,128)(2,1)} %tv_ref.1, s32[4,1,32]{2,1,0:T(1,128)} %bitcast.9, bf16[4,1,4096,128]{3,2,1,0:T(8,128)(2,1)} %ck_ref.1, ...), custom_call_target="tpu_custom_call" | custom-call | tf_op jit(solution)/shard_map/pallas_call | solution.py:135
  16.3 74.3 %shard_map.137 = bf16[32,2048]{1,0:T(8,128)(2,1)} custom-call(bf16[128,2048]{1,0:T(8,128)(2,1)} %shard_map.136.part_ref, bf16[32,2048]{1,0:T(8,128)(2,1)} %hid_ref.1, f32[1,2048]{1,0:T(1,128)} %bitcast.6, s32[8,32]{1,0:T(8,128)} %bitcast.7, f32[8,32]{1,0:T(8,128)} %bitcast.8, bf16[1,2048,1536]{2,1,0:T(8,128)(2,1)} %gu_hbm.1, bf16[1,768,2048]{2,1,0:T(8,128)(2,1)} %dn_hbm.1), custom_call_target="tpu_custom_call" | custom-call | tf_op jit(solution)/shard_map/pallas_call | solution.py:410
  90.5 1.6 %copy.17 = bf16[32,2048]{1,0:T(8,128)(2,1)} copy(bf16[32,2048]{1,0:T(8,128)(2,1)} %shard_map.137) | data formatting | bytes 262144
